TPU v7x, 32 devices: a whole 2x2x4 slice. The times are simulated.
32 devices in a mesh: section: 4 (over y, x), seq: 8 (over z, core).
Axes of the slice: x: 2, y: 2, z: 4, core: 2. Of those that a mesh axis runs over, the one named last changes fastest.
Arguments:
- inflow: bfloat16 [4, 512, 4096], P('section', 'seq'), may hold values from -6 to 6
- fresh: bfloat16 [1, 512, 4096], P(None, 'seq'), may hold values from -6 to 6
- proj_weight: bfloat16 [4, 4096, 640], P('section'), may hold values from -0.09375 to 0.09375
- xz_weight: bfloat16 [4, 4096, 2, 4096], P('section', None, None, 'seq'), may hold values from -0.09375 to 0.09375
- conv_weight: float32 [4, 4, 4608], P('section'), may hold values from -3 to 3
- conv_bias: float32 [4, 4608], P('section'), may hold values from -3 to 3
- step_bias: float32 [4, 128], P('section'), may hold values from -3 to 0
- decay_log: float32 [4, 128], P('section'), may hold values from -7 to -1
- skip_weight: float32 [4, 128], P('section'), may hold values from 0.5 to 1.5
- norm_gain: float32 [4, 4096], P('section'), may hold values from 0.5 to 1.5
- out_weight: bfloat16 [4, 4096, 4096], P('section', 'seq'), may hold values from -0.09375 to 0.09375
Outputs:
- section_outputs: float32 [4, 2, 512, 4096], P('section', None, 'seq')
All inputs are finite; a program needn't handle non-finite values.
Results may differ from a plain program's by a relative error of at most 0.014.
Values may be sent and summed in bfloat16 or wider, within the bound.
No kernel may reach another device: no remote copies, remote signals or barrier semaphores. Data moves between devices by JAX's collectives and lax.ppermute only.
A program may use at most 128 MiB of HBM per device.

v0:
```python
import jax
import jax.numpy as jnp
from jax import lax
from jax.sharding import PartitionSpec as P

HEADS = 128
HEAD_DIM = 32
STATE = 64
GROUPS = 4
CONV = 4
BLOCK = 128


def shifted(value, axis, steps):
    count = lax.axis_size(axis)
    leading, last = (max(0, -steps), min(count, count - steps))
    return lax.ppermute(value, axis, [(source, source + steps) for source in range(leading, last)])


def run_block(state, pieces):
    x_block, b_block, c_block, step_block, decay_block = pieces
    cumulus = jnp.cumsum(decay_block, axis=0)
    scores = jnp.einsum("qgn,kgn->gqk", c_block, b_block, preferred_element_type=jnp.float32)
    along = jnp.moveaxis(cumulus, 0, 2)
    row_count = cumulus.shape[0]
    row_index = lax.broadcasted_iota(jnp.int32, (row_count, row_count), 0)
    col_index = lax.broadcasted_iota(jnp.int32, (row_count, row_count), 1)
    log_gap = jnp.where(row_index >= col_index, along[..., :, None] - along[..., None, :], -1e30)
    step_along = jnp.moveaxis(step_block, 0, 2)
    mixing = (scores[:, None] * jnp.exp(log_gap) * step_along[..., None, :]).astype(jnp.bfloat16)
    diagonal_out = jnp.einsum(
        "gjqk,kgjp->qgjp", mixing, x_block, preferred_element_type=jnp.float32
    )
    block_total = cumulus[-1]
    weighted = (
        x_block.astype(jnp.float32) * (jnp.exp(block_total[None] - cumulus) * step_block)[..., None]
    ).astype(jnp.bfloat16)
    block_state = jnp.einsum(
        "kgjp,kgn->gjpn", weighted, b_block, preferred_element_type=jnp.float32
    )
    entering = state.astype(jnp.bfloat16)
    off_out = (
        jnp.einsum("qgn,gjpn->qgjp", c_block, entering, preferred_element_type=jnp.float32)
        * jnp.exp(cumulus)[..., None]
    )
    new_state = jnp.exp(block_total)[..., None, None] * state + block_state
    return (new_state, diagonal_out + off_out)


def on_device(
    inflow,
    fresh,
    proj_weight,
    xz_weight,
    conv_weight,
    conv_bias,
    step_bias,
    decay_log,
    skip_weight,
    norm_gain,
    out_weight,
):
    group_size = lax.axis_size("seq")
    position = lax.axis_index("section")
    member = lax.axis_index("seq")
    tokens, width = (inflow.shape[1], inflow.shape[2])
    length = tokens * group_size
    inner = HEADS * HEAD_DIM
    heads_dev = HEADS // group_size
    chan_dev = heads_dev * HEAD_DIM
    bc_width = GROUPS * STATE
    per_group = HEADS // GROUPS
    head_start = member * heads_dev
    group_index = head_start // per_group
    b_start = group_index * STATE
    c_start = bc_width + group_index * STATE
    dt_start = 2 * bc_width + head_start
    xz_local = xz_weight[0].reshape(width, 2 * chan_dev)
    full_proj = proj_weight[0]

    def own_channels(table):
        last = table.ndim - 1
        return jnp.concatenate(
            [
                lax.dynamic_slice_in_dim(table, head_start * HEAD_DIM, chan_dev, last),
                lax.dynamic_slice_in_dim(table, inner + b_start, STATE, last),
                lax.dynamic_slice_in_dim(table, inner + c_start, STATE, last),
            ],
            axis=last,
        )

    taps_own = own_channels(conv_weight[0])
    offset_own = own_channels(conv_bias[0])
    bias_own = lax.dynamic_slice_in_dim(step_bias[0], head_start, heads_dev)
    rate_own = -jnp.exp(lax.dynamic_slice_in_dim(decay_log[0], head_start, heads_dev))
    skip_own = lax.dynamic_slice_in_dim(skip_weight[0], head_start, heads_dev)
    gain_own = lax.dynamic_slice_in_dim(norm_gain[0], head_start * HEAD_DIM, chan_dev)
    out_local = out_weight[0]
    group_mask = (lax.broadcasted_iota(jnp.int32, (GROUPS, 1), 0) == group_index).astype(
        jnp.float32
    )
    own_weight = jnp.concatenate(
        [
            xz_local,
            lax.dynamic_slice_in_dim(full_proj, b_start, STATE, 1),
            lax.dynamic_slice_in_dim(full_proj, c_start, STATE, 1),
            lax.dynamic_slice_in_dim(full_proj, dt_start, heads_dev, 1),
        ],
        axis=1,
    )

    def layer(shard):
        projected = jnp.dot(
            lax.all_gather(shard, "seq", axis=0, tiled=True),
            own_weight,
            preferred_element_type=jnp.float32,
        ).astype(jnp.bfloat16)
        gate_z = projected[:, :chan_dev]
        joined = projected[:, chan_dev : 2 * chan_dev + 2 * STATE]
        padded = jnp.concatenate(
            [jnp.zeros((CONV - 1, joined.shape[1]), jnp.bfloat16), joined], axis=0
        )
        conv_sum = offset_own + taps_own[0] * padded[0:length].astype(jnp.float32)
        for offset in range(1, CONV):
            conv_sum = conv_sum + taps_own[offset] * padded[offset : offset + length].astype(
                jnp.float32
            )
        convolved = jax.nn.silu(conv_sum).astype(jnp.bfloat16)
        block_count = length // BLOCK
        x_part = convolved[:, :chan_dev]
        x_blocks = x_part.reshape(block_count, BLOCK, 1, heads_dev, HEAD_DIM)
        b_blocks = convolved[:, chan_dev : chan_dev + STATE].reshape(block_count, BLOCK, 1, STATE)
        c_blocks = convolved[:, chan_dev + STATE :].reshape(block_count, BLOCK, 1, STATE)
        step_size = jax.nn.softplus(
            projected[:, 2 * chan_dev + 2 * STATE :].astype(jnp.float32) + bias_own
        )
        log_decay = rate_own * step_size
        step_blocks = step_size.reshape(block_count, BLOCK, 1, heads_dev)
        decay_blocks = log_decay.reshape(block_count, BLOCK, 1, heads_dev)
        start_state = jnp.zeros((1, heads_dev, HEAD_DIM, STATE), jnp.float32)
        _, scanned = lax.scan(
            run_block, start_state, (x_blocks, b_blocks, c_blocks, step_blocks, decay_blocks)
        )
        mixed = scanned.reshape(length, heads_dev, HEAD_DIM) + skip_own[:, None] * x_part.reshape(
            length, heads_dev, HEAD_DIM
        ).astype(jnp.float32)
        gated = mixed.reshape(length, chan_dev) * jax.nn.silu(gate_z.astype(jnp.float32))
        own_squares = jnp.sum(gated * gated, axis=1)
        summed_squares = lax.psum(group_mask * own_squares[None, :], "seq")
        mean_square = jnp.sum(summed_squares * group_mask, axis=0) / (inner // GROUPS)
        normed = (gated * lax.rsqrt(mean_square + 1e-05)[:, None] * gain_own).astype(jnp.bfloat16)
        return lax.psum_scatter(
            jnp.dot(normed, out_local, preferred_element_type=jnp.float32),
            "seq",
            scatter_dimension=0,
            tiled=True,
        )

    results = [layer(inflow[0])]
    passed = shifted(results[-1].astype(jnp.bfloat16), "section", 1)
    entering_rows = jnp.where(position == 0, fresh[0], passed)
    results.append(layer(entering_rows))
    return jnp.stack(results)[None]


def solution(mesh):
    placed = (
        P("section", "seq", None),
        P(None, "seq", None),
        P("section", None, None),
        P("section", None, None, "seq"),
        P("section", None, None),
        P("section", None),
        P("section", None),
        P("section", None),
        P("section", None),
        P("section", None),
        P("section", "seq", None),
    )
    return jax.shard_map(
        on_device,
        mesh=mesh,
        in_specs=placed,
        out_specs=P("section", None, "seq", None),
        check_vma=False,
    )
```

profile of v0, /device:TPU:0, one launch (start us, length us, event | category | flops | bytes accessed | tf_op | source)
XLA Modules:
  0.0 464.4 jit_solution(18057231383627719839)
XLA Ops:
  7.4 9.4 %copy.88 = bf16[512,8,2,512]{3,1,2,0:T(8,128)(2,1)} copy(bf16[512,8,2,512]{3,2,1,0:T(2,128)(2,1)} %bitcast.287) | data formatting | bytes 16777216
  21.8 15.5 %concatenate.15 = bf16[4096,1168]{1,0:T(8,128)(2,1)} concatenate(bf16[4096,1024]{1,0:T(8,128)(2,1)} %bitcast.282, bf16[4096,64]{1,0:T(8,128)(2,1)S(1)} %get-tuple-element.240, bf16[4096,64]{1,0:T(8,128)(2,1)S(1)} %get-tuple-element.239, bf16[4096,16]{1,0:T(8,128)(2,1)S(1)} %dynamic-slice_bitcast_fusion), dimensions={1} | concatenate | bytes 19136512 | tf_op jit(solution)/shard_map/concatenate | solution.py:102
  41.7 16.9 %all-gather.6.cloned.1.call-done = bf16[1,512,4096]{2,1,0:T(8,128)(2,1)} async-done(((bf16[1,64,4096]{2,1,0:T(8,128)(2,1)}), bf16[1,512,4096]{2,1,0:T(8,128)(2,1)}) %all-gather.6.cloned.1.call-update) | async-done | bytes 4194320 | tf_op jit(solution)/shard_map/all_gather | solution.py:114
  58.6 10.6 %fusion.79 = bf16[512,1168]{0,1:T(8,128)(2,1)S(1)} fusion(bf16[4096,1168]{1,0:T(8,128)(2,1)} %concatenate.15, bf16[1,512,4096]{2,1,0:T(8,128)(2,1)} %all-gather.6.cloned.1.call-done), kind=kOutput, calls=%fused_computation.96 | convolution fusion | flops 4899545088 | bytes 14958592 | tf_op jit(solution)/shard_map/dot_general | solution.py:113
  73.2 38.5 %while.26 = (s32[]{:T(128)}, f32[1,16,32,64]{3,2,1,0:T(8,128)S(1)}, f32[4,128,1,16,32]{1,0,4,3,2:T(4,128)S(1)}, f32[4,128,1,16]{3,1,2,0:T(8,128)}, bf16[4,128,1,...) while((s32[]{:T(128)}, f32[1,16,32,64]{3,2,1,0:T(8,128)S(1)}, ...), condition=%wide.region_2.3_spmd.clone, body=%wide.region_0.2_spmd.clone.sunk | while | flops 37701632 | bytes 2641344 | solution.py:141
  77.3 5.3 %dynamic_update_slice.11 = f32[4,128,1,16,32]{1,0,4,3,2:T(4,128)S(1)} dynamic-update-slice(f32[4,128,1,16,32]{1,0,4,3,2:T(4,128)S(1)} %get-tuple-element.377, f32[1,128,1,16,32]{1,0,4,3,2:T(1,128)S(1)} %bitcast.288, s32[]{:T(128)} %get-tuple-element.375, s32[]{:T(128)} %constant.98.clone.1..sunk, s32[]{:T(128)} %constant.98.clone.1..sunk, s32[]{:T(128)} %constant.98.clone.1..sunk, ...) | dynamic-update-slice | bytes 524292 | tf_op jit(solution)/shard_map/while/body/jit(dynamic_update_index_in_dim)/dynamic_update_slice | solution.py:141
  86.9 5.3 %dynamic_update_slice.11 = f32[4,128,1,16,32]{1,0,4,3,2:T(4,128)S(1)} dynamic-update-slice(f32[4,128,1,16,32]{1,0,4,3,2:T(4,128)S(1)} %get-tuple-element.377, f32[1,128,1,16,32]{1,0,4,3,2:T(1,128)S(1)} %bitcast.288, s32[]{:T(128)} %get-tuple-element.375, s32[]{:T(128)} %constant.98.clone.1..sunk, s32[]{:T(128)} %constant.98.clone.1..sunk, s32[]{:T(128)} %constant.98.clone.1..sunk, ...) | dynamic-update-slice | bytes 524292 | tf_op jit(solution)/shard_map/while/body/jit(dynamic_update_index_in_dim)/dynamic_update_slice | solution.py:141
  96.5 5.3 %dynamic_update_slice.11 = f32[4,128,1,16,32]{1,0,4,3,2:T(4,128)S(1)} dynamic-update-slice(f32[4,128,1,16,32]{1,0,4,3,2:T(4,128)S(1)} %get-tuple-element.377, f32[1,128,1,16,32]{1,0,4,3,2:T(1,128)S(1)} %bitcast.288, s32[]{:T(128)} %get-tuple-element.375, s32[]{:T(128)} %constant.98.clone.1..sunk, s32[]{:T(128)} %constant.98.clone.1..sunk, s32[]{:T(128)} %constant.98.clone.1..sunk, ...) | dynamic-update-slice | bytes 524292 | tf_op jit(solution)/shard_map/while/body/jit(dynamic_update_index_in_dim)/dynamic_update_slice | solution.py:141
  106.2 5.3 %dynamic_update_slice.11 = f32[4,128,1,16,32]{1,0,4,3,2:T(4,128)S(1)} dynamic-update-slice(f32[4,128,1,16,32]{1,0,4,3,2:T(4,128)S(1)} %get-tuple-element.377, f32[1,128,1,16,32]{1,0,4,3,2:T(1,128)S(1)} %bitcast.288, s32[]{:T(128)} %get-tuple-element.375, s32[]{:T(128)} %constant.98.clone.1..sunk, s32[]{:T(128)} %constant.98.clone.1..sunk, s32[]{:T(128)} %constant.98.clone.1..sunk, ...) | dynamic-update-slice | bytes 524292 | tf_op jit(solution)/shard_map/while/body/jit(dynamic_update_index_in_dim)/dynamic_update_slice | solution.py:141
  113.3 15.2 %psum.14 = f32[4,512]{1,0:T(4,128)S(1)} all-reduce(f32[4,512]{1,0:T(4,128)S(1)} %broadcast_multiply_fusion.3), channel_id=1, replica_groups=mesh['section'=4,'seq'=8] {'seq'}, use_global_device_ids=true, to_apply=%region_4.5 | all-reduce | flops 2048 | bytes 16384 | tf_op jit(solution)/shard_map/psum | solution.py:149
  128.7 8.0 %fusion.72 = f32[512,4096]{1,0:T(8,128)} fusion(bf16[1,512,4096]{2,1,0:T(8,128)(2,1)} %param.25, f32[512,512]{0,1:T(8,128)S(1)} %get-tuple-element.236, f32[512]{0:T(512)S(1)} %bitcast.300, f32[512]{0:T(512)S(1)} %add_rsqrt_fusion.1), kind=kOutput, calls=%fused_computation.90 | convolution fusion | flops 2148270080 | bytes 13635584 | tf_op jit(solution)/shard_map/dot_general | solution.py:153
  136.7 87.5 %reduce-scatter.3.cloned.1.call-done = f32[64,4096]{1,0:T(8,128)} async-done(((f32[512,4096]{1,0:T(8,128)}), f32[64,4096]{1,0:T(8,128)}) %reduce-scatter.3.cloned.1.call-update) | async-done | bytes 1048592 | tf_op jit(solution)/shard_map/reduce_scatter | solution.py:152
  225.5 3.4 collective-permute-start
  228.9 9.2 %collective-permute-done = bf16[64,4096]{1,0:T(8,128)(2,1)S(1)} collective-permute-done((bf16[64,4096]{1,0:T(8,128)(2,1)S(1)}, bf16[64,4096]{1,0:T(8,128)(2,1)S(1)}, u32[]{:S(2)}, u32[]{:S(2)}) %collective-permute-start) | collective-permute-done | bytes 524320 | tf_op jit(solution)/shard_map/ppermute | solution.py:17
  239.1 48.3 %all-gather.4.cloned.1.call-done = bf16[512,4096]{1,0:T(8,128)(2,1)} async-done(((bf16[64,4096]{1,0:T(8,128)(2,1)}), bf16[512,4096]{1,0:T(8,128)(2,1)}) %all-gather.4.cloned.1.call-update) | async-done | bytes 4194320 | tf_op jit(solution)/shard_map/all_gather | solution.py:114
  287.4 12.7 %convolution_convert_fusion = bf16[512,1168]{0,1:T(8,128)(2,1)S(1)} fusion(bf16[512,4096]{1,0:T(8,128)(2,1)} %all-gather.4.cloned.1.call-done, bf16[4096,1168]{1,0:T(8,128)(2,1)} %concatenate.15), kind=kOutput, calls=%fused_computation.94 | convolution fusion | flops 4899545088 | bytes 14958592 | tf_op jit(solution)/shard_map/dot_general | solution.py:113
  304.2 38.5 %while.27 = (s32[]{:T(128)}, f32[1,16,32,64]{3,2,1,0:T(8,128)S(1)}, f32[4,128,1,16,32]{1,0,4,3,2:T(4,128)S(1)}, f32[4,128,1,16]{3,1,2,0:T(8,128)}, bf16[4,128,1,...) while((s32[]{:T(128)}, f32[1,16,32,64]{3,2,1,0:T(8,128)S(1)}, ...), condition=%wide.region_9.10_spmd.clone, body=%wide.region_7.9_spmd.clone.sunk | while | flops 37701632 | bytes 2641344 | solution.py:141
  308.2 5.3 %dynamic_update_slice.12 = f32[4,128,1,16,32]{1,0,4,3,2:T(4,128)S(1)} dynamic-update-slice(f32[4,128,1,16,32]{1,0,4,3,2:T(4,128)S(1)} %get-tuple-element.407, f32[1,128,1,16,32]{1,0,4,3,2:T(1,128)S(1)} %bitcast.289, s32[]{:T(128)} %get-tuple-element.405, s32[]{:T(128)} %constant.98.clone.1..sunk.1, s32[]{:T(128)} %constant.98.clone.1..sunk.1, s32[]{:T(128)} %constant.98.clone.1..sunk.1, ...) | dynamic-update-slice | bytes 524292 | tf_op jit(solution)/shard_map/while/body/jit(dynamic_update_index_in_dim)/dynamic_update_slice | solution.py:141
  317.8 5.3 %dynamic_update_slice.12 = f32[4,128,1,16,32]{1,0,4,3,2:T(4,128)S(1)} dynamic-update-slice(f32[4,128,1,16,32]{1,0,4,3,2:T(4,128)S(1)} %get-tuple-element.407, f32[1,128,1,16,32]{1,0,4,3,2:T(1,128)S(1)} %bitcast.289, s32[]{:T(128)} %get-tuple-element.405, s32[]{:T(128)} %constant.98.clone.1..sunk.1, s32[]{:T(128)} %constant.98.clone.1..sunk.1, s32[]{:T(128)} %constant.98.clone.1..sunk.1, ...) | dynamic-update-slice | bytes 524292 | tf_op jit(solution)/shard_map/while/body/jit(dynamic_update_index_in_dim)/dynamic_update_slice | solution.py:141
  327.5 5.3 %dynamic_update_slice.12 = f32[4,128,1,16,32]{1,0,4,3,2:T(4,128)S(1)} dynamic-update-slice(f32[4,128,1,16,32]{1,0,4,3,2:T(4,128)S(1)} %get-tuple-element.407, f32[1,128,1,16,32]{1,0,4,3,2:T(1,128)S(1)} %bitcast.289, s32[]{:T(128)} %get-tuple-element.405, s32[]{:T(128)} %constant.98.clone.1..sunk.1, s32[]{:T(128)} %constant.98.clone.1..sunk.1, s32[]{:T(128)} %constant.98.clone.1..sunk.1, ...) | dynamic-update-slice | bytes 524292 | tf_op jit(solution)/shard_map/while/body/jit(dynamic_update_index_in_dim)/dynamic_update_slice | solution.py:141
  337.1 5.3 %dynamic_update_slice.12 = f32[4,128,1,16,32]{1,0,4,3,2:T(4,128)S(1)} dynamic-update-slice(f32[4,128,1,16,32]{1,0,4,3,2:T(4,128)S(1)} %get-tuple-element.407, f32[1,128,1,16,32]{1,0,4,3,2:T(1,128)S(1)} %bitcast.289, s32[]{:T(128)} %get-tuple-element.405, s32[]{:T(128)} %constant.98.clone.1..sunk.1, s32[]{:T(128)} %constant.98.clone.1..sunk.1, s32[]{:T(128)} %constant.98.clone.1..sunk.1, ...) | dynamic-update-slice | bytes 524292 | tf_op jit(solution)/shard_map/while/body/jit(dynamic_update_index_in_dim)/dynamic_update_slice | solution.py:141
  344.3 15.2 %psum.15 = f32[4,512]{1,0:T(4,128)S(1)} all-reduce(f32[4,512]{1,0:T(4,128)S(1)} %broadcast_multiply_fusion.2), channel_id=1, replica_groups=mesh['section'=4,'seq'=8] {'seq'}, use_global_device_ids=true, to_apply=%region_11.12 | all-reduce | flops 2048 | bytes 16384 | tf_op jit(solution)/shard_map/psum | solution.py:149
  359.6 7.9 %fusion.70 = f32[512,4096]{1,0:T(8,128)} fusion(bf16[1,512,4096]{2,1,0:T(8,128)(2,1)} %param.25, f32[512,512]{0,1:T(8,128)S(1)} %get-tuple-element.234, f32[512]{0:T(512)S(1)} %add_rsqrt_fusion, f32[512]{0:T(512)S(1)} %bitcast.301), kind=kOutput, calls=%fused_computation.88 | convolution fusion | flops 2148270080 | bytes 13635584 | tf_op jit(solution)/shard_map/dot_general | solution.py:153
  367.6 87.6 %reduce-scatter.5.cloned.1.call-done = f32[64,4096]{1,0:T(8,128)} async-done(((f32[512,4096]{1,0:T(8,128)}), f32[64,4096]{1,0:T(8,128)}) %reduce-scatter.5.cloned.1.call-update) | async-done | bytes 1048592 | tf_op jit(solution)/shard_map/reduce_scatter | solution.py:152
  (230 shorter events, 60.5 us)
Async XLA Ops:
  6.5 32.8 %copy-start = (f32[1,4096]{1,0:T(1,128)S(1)}, f32[1,4096]{1,0:T(1,128)}, u32[]{:S(2)}) copy-start(f32[1,4096]{1,0:T(1,128)} %param.24) | copy-start | bytes 49156
  6.5 52.0 %all-gather.6.cloned.1.call-start = ((), (), s32[]{:S(2)}) async-start(), calls=%async_computation.5 | async-start | bytes 4718592 | tf_op jit(solution)/shard_map/all_gather | solution.py:114
  7.3 217.0 %reduce-scatter.3.cloned.1.call-start = ((), (), s32[]{:S(2)}) async-start(), calls=%async_computation.2 | async-start | bytes 9437184 | tf_op jit(solution)/shard_map/reduce_scatter | solution.py:152
  7.3 9.4 %copy-start.26 = (f32[1,128]{1,0:T(1,128)S(1)}, f32[1,128]{1,0:T(1,128)}, u32[]{:S(2)}) copy-start(f32[1,128]{1,0:T(1,128)} %param.23) | copy-start | bytes 1540
  21.8 16.1 %copy-start.24 = (f32[1,128]{1,0:T(1,128)S(1)}, f32[1,128]{1,0:T(1,128)}, u32[]{:S(2)}) copy-start(f32[1,128]{1,0:T(1,128)} %param.21) | copy-start | bytes 1540
  21.8 16.1 %copy-start.25 = (f32[1,128]{1,0:T(1,128)S(1)}, f32[1,128]{1,0:T(1,128)}, u32[]{:S(2)}) copy-start(f32[1,128]{1,0:T(1,128)} %param.22) | copy-start | bytes 1540
  37.9 33.2 %copy-start.20 = (f32[16]{0:T(128)}, f32[16]{0:T(128)S(1)}, u32[]{:S(2)}) copy-start(f32[16]{0:T(128)S(1)} %get-tuple-element.253) | copy-start | bytes 196
  37.9 33.2 %copy-start.22 = (f32[16]{0:T(128)}, f32[16]{0:T(128)S(1)}, u32[]{:S(2)}) copy-start(f32[16]{0:T(128)S(1)} %get-tuple-element.254) | copy-start | bytes 196
  40.8 28.4 %copy-start.8 = (f32[640]{0:T(1024)}, f32[640]{0:T(1024)S(1)}, u32[]{:S(2)}) copy-start(f32[640]{0:T(1024)S(1)} %pad_maximum_fusion.1) | copy-start | bytes 7684
  41.6 27.6 %copy-start.10 = (f32[640]{0:T(1024)}, f32[640]{0:T(1024)S(1)}, u32[]{:S(2)}) copy-start(f32[640]{0:T(1024)S(1)} %get-tuple-element.193) | copy-start | bytes 7684
  41.6 27.6 %copy-start.12 = (f32[640]{0:T(1024)}, f32[640]{0:T(1024)S(1)}, u32[]{:S(2)}) copy-start(f32[640]{0:T(1024)S(1)} %get-tuple-element.194) | copy-start | bytes 7684
  41.6 27.6 %copy-start.14 = (f32[640]{0:T(1024)}, f32[640]{0:T(1024)S(1)}, u32[]{:S(2)}) copy-start(f32[640]{0:T(1024)S(1)} %get-tuple-element.195) | copy-start | bytes 7684
  41.6 27.6 %copy-start.16 = (f32[640]{0:T(1024)}, f32[640]{0:T(1024)S(1)}, u32[]{:S(2)}) copy-start(f32[640]{0:T(1024)S(1)} %get-tuple-element.196) | copy-start | bytes 7684
  69.1 1.7 copy-start.4
  111.7 16.9 %copy-start.6 = (f32[1,512]{1,0:T(1,128)S(1)}, f32[1,512]{1,0:T(1,128)}, u32[]{:S(2)}) copy-start(f32[1,512]{1,0:T(1,128)} %constant_dynamic-slice_fusion.4) | copy-start | bytes 6148
  136.7 101.5 %copy-start.5 = (bf16[1,64,4096]{2,1,0:T(8,128)(2,1)S(1)}, bf16[1,64,4096]{2,1,0:T(8,128)(2,1)}, u32[]{:S(2)}) copy-start(bf16[1,64,4096]{2,1,0:T(8,128)(2,1)} %param.16) | copy-start | bytes 1572868
  136.7 150.8 %all-gather.4.cloned.1.call-start = ((), (), s32[]{:S(2)}) async-start(), calls=%async_computation.3 | async-start | bytes 4718592 | tf_op jit(solution)/shard_map/all_gather | solution.py:114
  225.5 12.7 %collective-permute-start = (bf16[64,4096]{1,0:T(8,128)(2,1)S(1)}, bf16[64,4096]{1,0:T(8,128)(2,1)S(1)}, u32[]{:S(2)}, u32[]{:S(2)}) collective-permute-start(bf16[64,4096]{1,0:T(8,128)(2,1)S(1)} %convert_element_type.138), channel_id=1, source_target_pairs={{0,8},{8,16},{16,24},{1,9},{9,17},{17,25},{2,10},{10,18},{18,26},{... | collective-permute-start | bytes 1572872 | tf_op jit(solution)/shard_map/ppermute | solution.py:17
  239.1 216.1 %reduce-scatter.5.cloned.1.call-start = ((), (), s32[]{:S(2)}) async-start(), calls=%async_computation.4 | async-start | bytes 9437184 | tf_op jit(solution)/shard_map/reduce_scatter | solution.py:152
  300.2 2.4 copy-start.3
  300.9 1.6 copy-start.23
  342.7 16.9 %copy-start.7 = (f32[1,512]{1,0:T(1,128)S(1)}, f32[1,512]{1,0:T(1,128)}, u32[]{:S(2)}) copy-start(f32[1,512]{1,0:T(1,128)} %constant_dynamic-slice_fusion.4) | copy-start | bytes 6148
  367.5 87.6 %copy-start.2 = (f32[64,4096]{1,0:T(8,128)S(1)}, f32[64,4096]{1,0:T(8,128)}, u32[]{:S(2)}) copy-start(f32[64,4096]{1,0:T(8,128)} %reduce-scatter.3.cloned.1.call-done) | copy-start | bytes 3145732
  455.1 2.7 copy-start.1
  (8 other events, 8.2 us)
Sparse Core Ops, SparseCore 0:
  8.9 49.5 all-gather.5
  136.8 87.4 reduce-scatter.2
  239.2 48.2 all-gather.3
  367.7 87.4 reduce-scatter.4
where the time goes:
time: 466 us; the launch traced here: 464 us
  waiting for transfers between devices  250 us (54%)
  local copies, waits for them, and re-layouts  97.7 us (21%)
  matrix products  53.9 us (12%)
  blocking collectives  30.5 us (7%)
  other arithmetic  14.3 us (3%)
  between operations  13.7 us (3%)
    reduce_scatter x2, waiting for transfers between devices, layer(): lax.psum_scatter(jnp.dot(normed, out_local, preferred_element_type=jnp.fl...  175 us
    all_gather x2, waiting for transfers between devices, layer(): lax.all_gather(shard, 'seq', axis=0, tiled=True)  65.2 us
    dynamic_update_slice x8, local copies, waits for them, and re-layouts, layer(): lax.scan(run_block, start_state, (x_blocks, b_blocks, c_blocks, step_bloc...  42.2 us
    psum x2, blocking collectives, layer(): summed_squares = lax.psum(group_mask * own_squares[None, :], 'seq')  30.5 us
    dot_general x2, matrix products, layer(): jnp.dot(lax.all_gather(shard, 'seq', axis=0, tiled=True), own_weight, pre...  23.3 us
    dot_general x2, matrix products, layer(): jnp.dot(normed, out_local, preferred_element_type=jnp.float32)  15.9 us
    concatenate x1, local copies, waits for them, and re-layouts, on_device(): jnp.concatenate([xz_local, lax.dynamic_slice_in_dim(full_proj, b_start, S...  15.5 us
    unnamed x65, local copies, waits for them, and re-layouts  12.3 us
  transfers between devices with their start and end apart: 5, of which 5 were waited for; matrix products, arithmetic and copies ran while one was open for 7% of the time, Pallas kernels for 0%

commit v1 on v0

--- a/solution.py
+++ b/solution.py
@@ -146,7 +146,9 @@
         ).astype(jnp.float32)
         gated = mixed.reshape(length, chan_dev) * jax.nn.silu(gate_z.astype(jnp.float32))
         own_squares = jnp.sum(gated * gated, axis=1)
-        summed_squares = lax.psum(group_mask * own_squares[None, :], "seq")
+        own = group_mask * own_squares[None, :]
+        parts = lax.all_gather(own, "seq")
+        summed_squares = jnp.sum(parts, axis=0)
         mean_square = jnp.sum(summed_squares * group_mask, axis=0) / (inner // GROUPS)
         normed = (gated * lax.rsqrt(mean_square + 1e-05)[:, None] * gain_own).astype(jnp.bfloat16)
         return lax.psum_scatter(

time: 466 us -> 466 us (level)
    psum x2 -> x0, blocking collectives: 30.5 us -> none  [layer(): summed_squares = lax.psum(group_mask * own_squares[None, :], 'seq')]
    all_gather x0 -> x2, blocking collectives: none -> 28.4 us  [layer(): parts = lax.all_gather(own, 'seq')]
where the time goes in v1:
time: 466 us; the launch traced here: 464 us
  waiting for transfers between devices  252 us (54%)
  local copies, waits for them, and re-layouts  97.7 us (21%)
  matrix products  53.9 us (12%)
  blocking collectives  28.4 us (6%)
  other arithmetic  14.4 us (3%)
  between operations  13.7 us (3%)
    reduce_scatter x2, waiting for transfers between devices, layer(): lax.psum_scatter(jnp.dot(normed, out_local, preferred_element_type=jnp.fl...  177 us
    all_gather x2, waiting for transfers between devices, layer(): lax.all_gather(shard, 'seq', axis=0, tiled=True)  65.2 us
    dynamic_update_slice x8, local copies, waits for them, and re-layouts, layer(): lax.scan(run_block, start_state, (x_blocks, b_blocks, c_blocks, step_bloc...  42.2 us
    all_gather x2, blocking collectives, layer(): parts = lax.all_gather(own, 'seq')  28.4 us
    dot_general x2, matrix products, layer(): jnp.dot(lax.all_gather(shard, 'seq', axis=0, tiled=True), own_weight, pre...  23.3 us
    dot_general x2, matrix products, layer(): jnp.dot(normed, out_local, preferred_element_type=jnp.float32)  15.9 us
    concatenate x1, local copies, waits for them, and re-layouts, on_device(): jnp.concatenate([xz_local, lax.dynamic_slice_in_dim(full_proj, b_start, S...  15.5 us
    unnamed x65, local copies, waits for them, and re-layouts  12.3 us
  transfers between devices with their start and end apart: 5, of which 5 were waited for; matrix products, arithmetic and copies ran while one was open for 7% of the time, Pallas kernels for 0%

profile of v1, /device:TPU:0, one launch (start us, length us, event | category | flops | bytes accessed | tf_op | source)
XLA Modules:
  0.0 464.0 jit_solution(17039927147991801097)
XLA Ops:
  7.4 9.4 %copy.112 = bf16[512,8,2,512]{3,1,2,0:T(8,128)(2,1)} copy(bf16[512,8,2,512]{3,2,1,0:T(2,128)(2,1)} %bitcast.287) | data formatting | bytes 16777216
  21.8 15.5 %concatenate.15 = bf16[4096,1168]{1,0:T(8,128)(2,1)} concatenate(bf16[4096,1024]{1,0:T(8,128)(2,1)} %bitcast.282, bf16[4096,64]{1,0:T(8,128)(2,1)S(1)} %get-tuple-element.256, bf16[4096,64]{1,0:T(8,128)(2,1)S(1)} %get-tuple-element.255, bf16[4096,16]{1,0:T(8,128)(2,1)S(1)} %dynamic-slice_bitcast_fusion), dimensions={1} | concatenate | bytes 19136512 | tf_op jit(solution)/shard_map/concatenate | solution.py:102
  41.7 16.9 %all-gather.6.cloned.1.call-done = bf16[1,512,4096]{2,1,0:T(8,128)(2,1)} async-done(((bf16[1,64,4096]{2,1,0:T(8,128)(2,1)}), bf16[1,512,4096]{2,1,0:T(8,128)(2,1)}) %all-gather.6.cloned.1.call-update) | async-done | bytes 4194320 | tf_op jit(solution)/shard_map/all_gather | solution.py:114
  58.6 10.6 %fusion.79 = bf16[512,1168]{0,1:T(8,128)(2,1)S(1)} fusion(bf16[4096,1168]{1,0:T(8,128)(2,1)} %concatenate.15, bf16[1,512,4096]{2,1,0:T(8,128)(2,1)} %all-gather.6.cloned.1.call-done), kind=kOutput, calls=%fused_computation.96 | convolution fusion | flops 4899545088 | bytes 14958592 | tf_op jit(solution)/shard_map/dot_general | solution.py:113
  73.2 38.5 %while.26 = (s32[]{:T(128)}, f32[1,16,32,64]{3,2,1,0:T(8,128)S(1)}, f32[4,128,1,16,32]{1,0,4,3,2:T(4,128)S(1)}, f32[4,128,1,16]{3,1,2,0:T(8,128)}, bf16[4,128,1,...) while((s32[]{:T(128)}, f32[1,16,32,64]{3,2,1,0:T(8,128)S(1)}, ...), condition=%wide.region_2.3_spmd.clone, body=%wide.region_0.2_spmd.clone.sunk | while | flops 37701632 | bytes 2641344 | solution.py:141
  77.3 5.3 %dynamic_update_slice.11 = f32[4,128,1,16,32]{1,0,4,3,2:T(4,128)S(1)} dynamic-update-slice(f32[4,128,1,16,32]{1,0,4,3,2:T(4,128)S(1)} %get-tuple-element.393, f32[1,128,1,16,32]{1,0,4,3,2:T(1,128)S(1)} %bitcast.288, s32[]{:T(128)} %get-tuple-element.391, s32[]{:T(128)} %constant.98.clone.1..sunk, s32[]{:T(128)} %constant.98.clone.1..sunk, s32[]{:T(128)} %constant.98.clone.1..sunk, ...) | dynamic-update-slice | bytes 524292 | tf_op jit(solution)/shard_map/while/body/jit(dynamic_update_index_in_dim)/dynamic_update_slice | solution.py:141
  86.9 5.3 %dynamic_update_slice.11 = f32[4,128,1,16,32]{1,0,4,3,2:T(4,128)S(1)} dynamic-update-slice(f32[4,128,1,16,32]{1,0,4,3,2:T(4,128)S(1)} %get-tuple-element.393, f32[1,128,1,16,32]{1,0,4,3,2:T(1,128)S(1)} %bitcast.288, s32[]{:T(128)} %get-tuple-element.391, s32[]{:T(128)} %constant.98.clone.1..sunk, s32[]{:T(128)} %constant.98.clone.1..sunk, s32[]{:T(128)} %constant.98.clone.1..sunk, ...) | dynamic-update-slice | bytes 524292 | tf_op jit(solution)/shard_map/while/body/jit(dynamic_update_index_in_dim)/dynamic_update_slice | solution.py:141
  96.5 5.3 %dynamic_update_slice.11 = f32[4,128,1,16,32]{1,0,4,3,2:T(4,128)S(1)} dynamic-update-slice(f32[4,128,1,16,32]{1,0,4,3,2:T(4,128)S(1)} %get-tuple-element.393, f32[1,128,1,16,32]{1,0,4,3,2:T(1,128)S(1)} %bitcast.288, s32[]{:T(128)} %get-tuple-element.391, s32[]{:T(128)} %constant.98.clone.1..sunk, s32[]{:T(128)} %constant.98.clone.1..sunk, s32[]{:T(128)} %constant.98.clone.1..sunk, ...) | dynamic-update-slice | bytes 524292 | tf_op jit(solution)/shard_map/while/body/jit(dynamic_update_index_in_dim)/dynamic_update_slice | solution.py:141
  106.2 5.3 %dynamic_update_slice.11 = f32[4,128,1,16,32]{1,0,4,3,2:T(4,128)S(1)} dynamic-update-slice(f32[4,128,1,16,32]{1,0,4,3,2:T(4,128)S(1)} %get-tuple-element.393, f32[1,128,1,16,32]{1,0,4,3,2:T(1,128)S(1)} %bitcast.288, s32[]{:T(128)} %get-tuple-element.391, s32[]{:T(128)} %constant.98.clone.1..sunk, s32[]{:T(128)} %constant.98.clone.1..sunk, s32[]{:T(128)} %constant.98.clone.1..sunk, ...) | dynamic-update-slice | bytes 524292 | tf_op jit(solution)/shard_map/while/body/jit(dynamic_update_index_in_dim)/dynamic_update_slice | solution.py:141
  113.3 14.2 %all_gather.15 = f32[8,4,512]{2,1,0:T(4,128)S(1)} all-gather(f32[1,4,512]{2,1,0:T(4,128)S(1)} %broadcast_multiply_fusion.3), channel_id=1, replica_groups=mesh['section'=4,'seq'=8] {'seq'}, dimensions={0}, use_global_device_ids=true | all-gather | bytes 73728 | tf_op jit(solution)/shard_map/all_gather | solution.py:150
  127.6 8.0 %fusion.72 = f32[512,4096]{1,0:T(8,128)} fusion(bf16[1,512,4096]{2,1,0:T(8,128)(2,1)} %param.25, f32[512,512]{0,1:T(8,128)S(1)} %get-tuple-element.252, f32[512]{0:T(512)S(1)} %bitcast.300, f32[512]{0:T(512)S(1)} %add_rsqrt_fusion.1), kind=kOutput, calls=%fused_computation.90 | convolution fusion | flops 2148270080 | bytes 13635584 | tf_op jit(solution)/shard_map/dot_general | solution.py:155
  135.7 88.4 %reduce-scatter.3.cloned.1.call-done = f32[64,4096]{1,0:T(8,128)} async-done(((f32[512,4096]{1,0:T(8,128)}), f32[64,4096]{1,0:T(8,128)}) %reduce-scatter.3.cloned.1.call-update) | async-done | bytes 1048592 | tf_op jit(solution)/shard_map/reduce_scatter | solution.py:154
  225.3 3.4 collective-permute-start
  228.7 9.3 %collective-permute-done = bf16[64,4096]{1,0:T(8,128)(2,1)S(1)} collective-permute-done((bf16[64,4096]{1,0:T(8,128)(2,1)S(1)}, bf16[64,4096]{1,0:T(8,128)(2,1)S(1)}, u32[]{:S(2)}, u32[]{:S(2)}) %collective-permute-start) | collective-permute-done | bytes 524320 | tf_op jit(solution)/shard_map/ppermute | solution.py:17
  238.9 48.3 %all-gather.4.cloned.1.call-done = bf16[512,4096]{1,0:T(8,128)(2,1)} async-done(((bf16[64,4096]{1,0:T(8,128)(2,1)}), bf16[512,4096]{1,0:T(8,128)(2,1)}) %all-gather.4.cloned.1.call-update) | async-done | bytes 4194320 | tf_op jit(solution)/shard_map/all_gather | solution.py:114
  287.2 12.7 %convolution_convert_fusion = bf16[512,1168]{0,1:T(8,128)(2,1)S(1)} fusion(bf16[512,4096]{1,0:T(8,128)(2,1)} %all-gather.4.cloned.1.call-done, bf16[4096,1168]{1,0:T(8,128)(2,1)} %concatenate.15), kind=kOutput, calls=%fused_computation.94 | convolution fusion | flops 4899545088 | bytes 14958592 | tf_op jit(solution)/shard_map/dot_general | solution.py:113
  304.0 38.5 %while.27 = (s32[]{:T(128)}, f32[1,16,32,64]{3,2,1,0:T(8,128)S(1)}, f32[4,128,1,16,32]{1,0,4,3,2:T(4,128)S(1)}, f32[4,128,1,16]{3,1,2,0:T(8,128)}, bf16[4,128,1,...) while((s32[]{:T(128)}, f32[1,16,32,64]{3,2,1,0:T(8,128)S(1)}, ...), condition=%wide.region_9.10_spmd.clone, body=%wide.region_7.9_spmd.clone.sunk | while | flops 37701632 | bytes 2641344 | solution.py:141
  308.0 5.3 %dynamic_update_slice.12 = f32[4,128,1,16,32]{1,0,4,3,2:T(4,128)S(1)} dynamic-update-slice(f32[4,128,1,16,32]{1,0,4,3,2:T(4,128)S(1)} %get-tuple-element.423, f32[1,128,1,16,32]{1,0,4,3,2:T(1,128)S(1)} %bitcast.289, s32[]{:T(128)} %get-tuple-element.421, s32[]{:T(128)} %constant.98.clone.1..sunk.1, s32[]{:T(128)} %constant.98.clone.1..sunk.1, s32[]{:T(128)} %constant.98.clone.1..sunk.1, ...) | dynamic-update-slice | bytes 524292 | tf_op jit(solution)/shard_map/while/body/jit(dynamic_update_index_in_dim)/dynamic_update_slice | solution.py:141
  317.6 5.3 %dynamic_update_slice.12 = f32[4,128,1,16,32]{1,0,4,3,2:T(4,128)S(1)} dynamic-update-slice(f32[4,128,1,16,32]{1,0,4,3,2:T(4,128)S(1)} %get-tuple-element.423, f32[1,128,1,16,32]{1,0,4,3,2:T(1,128)S(1)} %bitcast.289, s32[]{:T(128)} %get-tuple-element.421, s32[]{:T(128)} %constant.98.clone.1..sunk.1, s32[]{:T(128)} %constant.98.clone.1..sunk.1, s32[]{:T(128)} %constant.98.clone.1..sunk.1, ...) | dynamic-update-slice | bytes 524292 | tf_op jit(solution)/shard_map/while/body/jit(dynamic_update_index_in_dim)/dynamic_update_slice | solution.py:141
  327.3 5.3 %dynamic_update_slice.12 = f32[4,128,1,16,32]{1,0,4,3,2:T(4,128)S(1)} dynamic-update-slice(f32[4,128,1,16,32]{1,0,4,3,2:T(4,128)S(1)} %get-tuple-element.423, f32[1,128,1,16,32]{1,0,4,3,2:T(1,128)S(1)} %bitcast.289, s32[]{:T(128)} %get-tuple-element.421, s32[]{:T(128)} %constant.98.clone.1..sunk.1, s32[]{:T(128)} %constant.98.clone.1..sunk.1, s32[]{:T(128)} %constant.98.clone.1..sunk.1, ...) | dynamic-update-slice | bytes 524292 | tf_op jit(solution)/shard_map/while/body/jit(dynamic_update_index_in_dim)/dynamic_update_slice | solution.py:141
  336.9 5.3 %dynamic_update_slice.12 = f32[4,128,1,16,32]{1,0,4,3,2:T(4,128)S(1)} dynamic-update-slice(f32[4,128,1,16,32]{1,0,4,3,2:T(4,128)S(1)} %get-tuple-element.423, f32[1,128,1,16,32]{1,0,4,3,2:T(1,128)S(1)} %bitcast.289, s32[]{:T(128)} %get-tuple-element.421, s32[]{:T(128)} %constant.98.clone.1..sunk.1, s32[]{:T(128)} %constant.98.clone.1..sunk.1, s32[]{:T(128)} %constant.98.clone.1..sunk.1, ...) | dynamic-update-slice | bytes 524292 | tf_op jit(solution)/shard_map/while/body/jit(dynamic_update_index_in_dim)/dynamic_update_slice | solution.py:141
  344.1 14.2 %all_gather.17 = f32[8,4,512]{2,1,0:T(4,128)S(1)} all-gather(f32[1,4,512]{2,1,0:T(4,128)S(1)} %broadcast_multiply_fusion.2), channel_id=1, replica_groups=mesh['section'=4,'seq'=8] {'seq'}, dimensions={0}, use_global_device_ids=true | all-gather | bytes 73728 | tf_op jit(solution)/shard_map/all_gather | solution.py:150
  358.4 7.9 %fusion.70 = f32[512,4096]{1,0:T(8,128)} fusion(bf16[1,512,4096]{2,1,0:T(8,128)(2,1)} %param.25, f32[512,512]{0,1:T(8,128)S(1)} %get-tuple-element.250, f32[512]{0:T(512)S(1)} %add_rsqrt_fusion, f32[512]{0:T(512)S(1)} %bitcast.301), kind=kOutput, calls=%fused_computation.88 | convolution fusion | flops 2148270080 | bytes 13635584 | tf_op jit(solution)/shard_map/dot_general | solution.py:155
  366.3 88.4 %reduce-scatter.5.cloned.1.call-done = f32[64,4096]{1,0:T(8,128)} async-done(((f32[512,4096]{1,0:T(8,128)}), f32[64,4096]{1,0:T(8,128)}) %reduce-scatter.5.cloned.1.call-update) | async-done | bytes 1048592 | tf_op jit(solution)/shard_map/reduce_scatter | solution.py:154
  (232 shorter events, 60.6 us)
Async XLA Ops:
  6.5 32.8 %copy-start = (f32[1,4096]{1,0:T(1,128)S(1)}, f32[1,4096]{1,0:T(1,128)}, u32[]{:S(2)}) copy-start(f32[1,4096]{1,0:T(1,128)} %param.24) | copy-start | bytes 49156
  6.5 52.0 %all-gather.6.cloned.1.call-start = ((), (), s32[]{:S(2)}) async-start(), calls=%async_computation.5 | async-start | bytes 4718592 | tf_op jit(solution)/shard_map/all_gather | solution.py:114
  7.3 216.8 %reduce-scatter.3.cloned.1.call-start = ((), (), s32[]{:S(2)}) async-start(), calls=%async_computation.2 | async-start | bytes 9437184 | tf_op jit(solution)/shard_map/reduce_scatter | solution.py:154
  7.3 9.4 %copy-start.26 = (f32[1,128]{1,0:T(1,128)S(1)}, f32[1,128]{1,0:T(1,128)}, u32[]{:S(2)}) copy-start(f32[1,128]{1,0:T(1,128)} %param.23) | copy-start | bytes 1540
  21.8 16.1 %copy-start.24 = (f32[1,128]{1,0:T(1,128)S(1)}, f32[1,128]{1,0:T(1,128)}, u32[]{:S(2)}) copy-start(f32[1,128]{1,0:T(1,128)} %param.21) | copy-start | bytes 1540
  21.8 16.1 %copy-start.25 = (f32[1,128]{1,0:T(1,128)S(1)}, f32[1,128]{1,0:T(1,128)}, u32[]{:S(2)}) copy-start(f32[1,128]{1,0:T(1,128)} %param.22) | copy-start | bytes 1540
  37.9 33.2 %copy-start.20 = (f32[16]{0:T(128)}, f32[16]{0:T(128)S(1)}, u32[]{:S(2)}) copy-start(f32[16]{0:T(128)S(1)} %get-tuple-element.269) | copy-start | bytes 196
  37.9 33.2 %copy-start.22 = (f32[16]{0:T(128)}, f32[16]{0:T(128)S(1)}, u32[]{:S(2)}) copy-start(f32[16]{0:T(128)S(1)} %get-tuple-element.270) | copy-start | bytes 196
  40.8 28.4 %copy-start.8 = (f32[640]{0:T(1024)}, f32[640]{0:T(1024)S(1)}, u32[]{:S(2)}) copy-start(f32[640]{0:T(1024)S(1)} %pad_maximum_fusion.1) | copy-start | bytes 7684
  41.6 27.6 %copy-start.10 = (f32[640]{0:T(1024)}, f32[640]{0:T(1024)S(1)}, u32[]{:S(2)}) copy-start(f32[640]{0:T(1024)S(1)} %get-tuple-element.209) | copy-start | bytes 7684
  41.6 27.6 %copy-start.12 = (f32[640]{0:T(1024)}, f32[640]{0:T(1024)S(1)}, u32[]{:S(2)}) copy-start(f32[640]{0:T(1024)S(1)} %get-tuple-element.210) | copy-start | bytes 7684
  41.6 27.6 %copy-start.14 = (f32[640]{0:T(1024)}, f32[640]{0:T(1024)S(1)}, u32[]{:S(2)}) copy-start(f32[640]{0:T(1024)S(1)} %get-tuple-element.211) | copy-start | bytes 7684
  41.6 27.6 %copy-start.16 = (f32[640]{0:T(1024)}, f32[640]{0:T(1024)S(1)}, u32[]{:S(2)}) copy-start(f32[640]{0:T(1024)S(1)} %get-tuple-element.212) | copy-start | bytes 7684
  69.1 1.7 copy-start.4
  111.7 15.9 %copy-start.6 = (f32[1,512]{1,0:T(1,128)S(1)}, f32[1,512]{1,0:T(1,128)}, u32[]{:S(2)}) copy-start(f32[1,512]{1,0:T(1,128)} %constant_dynamic-slice_fusion.4) | copy-start | bytes 6148
  135.6 102.4 %copy-start.5 = (bf16[1,64,4096]{2,1,0:T(8,128)(2,1)S(1)}, bf16[1,64,4096]{2,1,0:T(8,128)(2,1)}, u32[]{:S(2)}) copy-start(bf16[1,64,4096]{2,1,0:T(8,128)(2,1)} %param.16) | copy-start | bytes 1572868
  135.6 151.6 %all-gather.4.cloned.1.call-start = ((), (), s32[]{:S(2)}) async-start(), calls=%async_computation.3 | async-start | bytes 4718592 | tf_op jit(solution)/shard_map/all_gather | solution.py:114
  225.3 12.7 %collective-permute-start = (bf16[64,4096]{1,0:T(8,128)(2,1)S(1)}, bf16[64,4096]{1,0:T(8,128)(2,1)S(1)}, u32[]{:S(2)}, u32[]{:S(2)}) collective-permute-start(bf16[64,4096]{1,0:T(8,128)(2,1)S(1)} %convert_element_type.138), channel_id=1, source_target_pairs={{0,8},{8,16},{16,24},{1,9},{9,17},{17,25},{2,10},{10,18},{18,26},{... | collective-permute-start | bytes 1572872 | tf_op jit(solution)/shard_map/ppermute | solution.py:17
  238.9 215.9 %reduce-scatter.5.cloned.1.call-start = ((), (), s32[]{:S(2)}) async-start(), calls=%async_computation.4 | async-start | bytes 9437184 | tf_op jit(solution)/shard_map/reduce_scatter | solution.py:154
  300.0 2.4 copy-start.3
  300.7 1.6 copy-start.23
  342.5 15.9 %copy-start.7 = (f32[1,512]{1,0:T(1,128)S(1)}, f32[1,512]{1,0:T(1,128)}, u32[]{:S(2)}) copy-start(f32[1,512]{1,0:T(1,128)} %constant_dynamic-slice_fusion.4) | copy-start | bytes 6148
  366.3 88.5 %copy-start.2 = (f32[64,4096]{1,0:T(8,128)S(1)}, f32[64,4096]{1,0:T(8,128)}, u32[]{:S(2)}) copy-start(f32[64,4096]{1,0:T(8,128)} %reduce-scatter.3.cloned.1.call-done) | copy-start | bytes 3145732
  454.7 2.7 copy-start.1
  (8 other events, 8.2 us)
Sparse Core Ops, SparseCore 0:
  8.9 49.5 all-gather.5
  135.7 88.2 reduce-scatter.2
  239.0 48.2 all-gather.3
  366.4 88.2 reduce-scatter.4
